TPU v7x, 256 devices: a whole 4x4x8 slice. The times are simulated.
256 devices in a mesh: pipe: 8 (over x, core), dp: 32 (over z, y).
Axes of the slice: x: 4, y: 4, z: 8, core: 2. Of those that a mesh axis runs over, the one named last changes fastest.
Arguments:
- x_ckpt: bfloat16 [8, 2, 32, 512, 512], P('pipe', None, 'dp'), may hold values from -6 to 6
- top_cot: bfloat16 [2, 32, 512, 512], P(None, 'dp'), may hold values from -6 to 6
- skip_cot: bfloat16 [2, 32, 512, 512], P(None, 'dp'), may hold values from -6 to 6
- w_conv: bfloat16 [8, 512, 3, 1024], P('pipe', 'dp'), may hold values from -0.15625 to 0.15625
- w_mix: bfloat16 [8, 512, 1024], P('pipe', 'dp'), may hold values from -0.25 to 0.25
Outputs:
- cot_inputs: bfloat16 [8, 2, 32, 512, 512], P('pipe', None, 'dp')
- grad_conv: float32 [8, 512, 3, 1024], P('pipe', 'dp')
- grad_mix: float32 [8, 512, 1024], P('pipe', 'dp')
All inputs are finite; a program needn't handle non-finite values.
Results may differ from a plain program's by a relative error of at most 0.014.
Values may be sent and summed in bfloat16 or wider, within the bound.
A program may use at most 128 MiB of HBM per device.

v0:
```python
import jax
import jax.numpy as jnp
from jax import lax
from jax.sharding import PartitionSpec as P


def passed_along(value, axis, steps):
    count = lax.axis_size(axis)
    leading, last = (max(0, -steps), min(count, count - steps))
    return lax.ppermute(value, axis, [(source, source + steps) for source in range(leading, last)])


def delay_seq(signal, shift_by):
    samples = signal.shape[1]
    rolled = jnp.roll(signal, shift_by, axis=1)
    positions = lax.broadcasted_iota(jnp.int32, (1, samples, 1), 1)
    return jnp.where(positions >= shift_by, rolled, jnp.zeros_like(rolled))


def advance_seq(signal, shift_by):
    samples = signal.shape[1]
    rolled = jnp.roll(signal, -shift_by, axis=1)
    positions = lax.broadcasted_iota(jnp.int32, (1, samples, 1), 1)
    return jnp.where(positions < samples - shift_by, rolled, jnp.zeros_like(rolled))


def tap_stack(signal, dilation):
    return jnp.stack([delay_seq(signal, offset * dilation) for offset in range(3)], axis=2)


def layer_back(x_rows, grad_next, skip_grad, conv_w, mix_w, dilation):
    channels = x_rows.shape[2]
    tapped_x = tap_stack(x_rows, dilation)
    pre_act = jnp.einsum("slkc,ckn->sln", tapped_x, conv_w, preferred_element_type=jnp.float32)
    filter_act = jnp.tanh(pre_act[..., :channels])
    gate_act = jax.nn.sigmoid(pre_act[..., channels:])
    hidden = (filter_act * gate_act).astype(jnp.bfloat16)
    cot_pair = jnp.concatenate([grad_next, skip_grad], axis=2)
    hid_grad = jnp.einsum("sln,cn->slc", cot_pair, mix_w, preferred_element_type=jnp.float32)
    pre_grad = jnp.concatenate(
        [
            hid_grad * gate_act * (1.0 - filter_act * filter_act),
            hid_grad * filter_act * gate_act * (1.0 - gate_act),
        ],
        axis=2,
    ).astype(jnp.bfloat16)
    back_taps = jnp.einsum("sln,ckn->slkc", pre_grad, conv_w, preferred_element_type=jnp.float32)
    input_grad = grad_next.astype(jnp.float32)
    for offset in range(3):
        input_grad = input_grad + advance_seq(back_taps[:, :, offset], offset * dilation)
    return (input_grad.astype(jnp.bfloat16), tapped_x, hidden, pre_grad, cot_pair)


def weight_terms(tapped_x, hidden, pre_grad, cot_pair):
    conv_term = jnp.einsum("slkc,sln->ckn", tapped_x, pre_grad, preferred_element_type=jnp.float32)
    mix_term = jnp.einsum("slc,sln->cn", hidden, cot_pair, preferred_element_type=jnp.float32)
    return jnp.concatenate([conv_term.reshape(conv_term.shape[0], -1), mix_term], axis=1)


def local(x_ckpt, top_cot, skip_cot, w_conv, w_mix):
    sec_count = lax.axis_size("pipe")
    sec_index = lax.axis_index("pipe")
    dilation = jnp.left_shift(jnp.int32(1), sec_index)
    conv_full, mix_full = (
        lax.all_gather(w_conv, "dp", axis=1, tiled=True),
        lax.all_gather(w_mix, "dp", axis=1, tiled=True),
    )
    conv_w = conv_full[0]
    mix_w = mix_full[0]
    micro_count, seq_count, samples, channels = x_ckpt.shape[1:]
    all_rows = micro_count * seq_count
    x_rows = x_ckpt[0].reshape(all_rows, samples, channels)
    top_rows = top_cot.reshape(all_rows, samples, channels)
    skip_rows = skip_cot.reshape(all_rows, samples, channels)
    is_last = sec_index == sec_count - 1
    blk_count = all_rows // seq_count
    step_count = sec_count + blk_count - 1
    act_shape = (seq_count, samples, channels)
    pair_shape = (seq_count, samples, 2 * channels)
    grad_init = jnp.zeros((channels, 8 * channels), jnp.float32)
    hid_init = jnp.zeros((1,), jnp.bfloat16)
    pre_init = jnp.zeros((1,), jnp.bfloat16)
    pair_init = jnp.zeros((1,), jnp.bfloat16)

    def step_fn(step_no, state_tuple):
        received, cot_store, grad_acc, hid_store, pre_store, pair_store = state_tuple
        blk_index = step_no - (sec_count - 1 - sec_index)
        is_active = (blk_index >= 0) & (blk_index < blk_count)
        row_start = jnp.clip(blk_index, 0, blk_count - 1) * seq_count
        x_blk = lax.dynamic_slice_in_dim(x_rows, row_start, seq_count, 0)
        top_blk = lax.dynamic_slice_in_dim(top_rows, row_start, seq_count, 0)
        skip_blk = lax.dynamic_slice_in_dim(skip_rows, row_start, seq_count, 0)
        grad_next = jnp.where(is_last, top_blk, received)

        def do_work(unused):
            input_grad, tapped_x, hidden, pre_grad, cot_pair = layer_back(
                x_blk, grad_next, skip_blk, conv_w, mix_w, dilation
            )
            grad_term = weight_terms(tapped_x, hidden, pre_grad, cot_pair)
            return (input_grad, hidden, pre_grad, cot_pair, grad_term)

        def no_work(unused):
            return (
                jnp.zeros(act_shape, jnp.bfloat16),
                jnp.zeros(act_shape, jnp.bfloat16),
                jnp.zeros(pair_shape, jnp.bfloat16),
                jnp.zeros(pair_shape, jnp.bfloat16),
                jnp.zeros_like(grad_acc),
            )

        input_grad, hidden, pre_grad, cot_pair, grad_term = lax.cond(is_active, do_work, no_work, 0)
        grad_acc = grad_acc + grad_term
        cot_store = jnp.where(
            is_active,
            lax.dynamic_update_slice_in_dim(cot_store, input_grad, row_start, 0),
            cot_store,
        )
        received = passed_along(input_grad, "pipe", -1)
        return (received, cot_store, grad_acc, hid_store, pre_store, pair_store)

    initial = (
        jnp.zeros(act_shape, jnp.bfloat16),
        jnp.zeros((all_rows, samples, channels), jnp.bfloat16),
        grad_init,
        hid_init,
        pre_init,
        pair_init,
    )
    final_state = lax.fori_loop(0, step_count, step_fn, initial)
    cot_store, grad_acc, hid_store, pre_store, pair_store = final_state[1:]
    shard_rows = channels // lax.axis_size("dp")
    shares = lax.psum_scatter(grad_acc, "dp", scatter_dimension=0, tiled=True)
    conv_share = shares[:, : 6 * channels].reshape(shard_rows, 3, 2 * channels)
    mix_share = shares[:, 6 * channels :]
    return (
        cot_store.reshape(1, micro_count, seq_count, samples, channels),
        conv_share[None],
        mix_share[None],
    )


def solution(mesh):
    placed = (
        P("pipe", None, "dp", None, None),
        P(None, "dp", None, None),
        P(None, "dp", None, None),
        P("pipe", "dp", None, None),
        P("pipe", "dp", None),
    )
    return jax.shard_map(
        local,
        mesh=mesh,
        in_specs=placed,
        out_specs=(
            P("pipe", None, "dp", None, None),
            P("pipe", "dp", None, None),
            P("pipe", "dp", None),
        ),
        check_vma=False,
    )
```

profile of v0, /device:TPU:8, one launch (start us, length us, event | category | flops | bytes accessed | tf_op | source)
XLA Modules:
  0.0 633.8 jit_solution(10756008087756776390)
XLA Ops:
  8.7 80.0 %all-gather.3.cloned.1.call-done = bf16[1,512,1024]{2,1,0:T(8,128)(2,1)} async-done(((bf16[1,16,1024]{2,1,0:T(8,128)(2,1)}), bf16[1,512,1024]{2,1,0:T(8,128)(2,1)}) %all-gather.3.cloned.1.call-update) | async-done | bytes 1048592 | tf_op jit(solution)/shard_map/all_gather | solution.py:66
  88.7 79.4 %all-gather.5.cloned.1.call-done = bf16[1,512,3,1024]{3,1,2,0:T(8,128)(2,1)} async-done(((bf16[1,16,3,1024]{3,1,2,0:T(8,128)(2,1)}), bf16[1,512,3,1024]{3,1,2,0:T(8,128)(2,1)}) %all-gather.5.cloned.1.call-update) | async-done | bytes 3145744 | tf_op jit(solution)/shard_map/all_gather | solution.py:65
  169.2 218.7 %while.20 = (s32[]{:T(128)}, bf16[1,512,512]{2,1,0:T(8,128)(2,1)S(1)}, bf16[2,512,512]{2,1,0:T(8,128)(2,1)}, f32[512,4096]{0,1:T(8,128)}, s32[]{:T(128)}, /*inde...) while((s32[]{:T(128)}, ...), condition=%wide.region_3.8_spmd.clone, body=%wide.region_0.7_spmd.clone.sunk | while | flops 5937039872 | bytes 117971056 | solution.py:129
  169.2 4.3 conditional.3
  169.3 4.3 broadcast.78
  173.6 1.3 collective-permute-start
  174.9 8.8 %select_add_fusion.2 = f32[512,4096]{0,1:T(8,128)} fusion(f32[512,4096]{0,1:T(8,128)} %get-tuple-element.522, f32[512,4096]{0,1:T(8,128)} %get-tuple-element.545, pred[]{:T(512)S(6)} %compare.5), kind=kLoop, calls=%fused_computation.59.clone.1 | loop fusion | flops 4194304 | bytes 25165824 | tf_op jit(solution)/shard_map/while/body/eval_jaxpr/add | solution.py:112
  184.9 4.3 conditional.3
  184.9 4.3 broadcast.78
  189.2 1.3 collective-permute-start
  190.5 11.2 %select_add_fusion.2 = f32[512,4096]{0,1:T(8,128)} fusion(f32[512,4096]{0,1:T(8,128)} %get-tuple-element.522, f32[512,4096]{0,1:T(8,128)} %get-tuple-element.545, pred[]{:T(512)S(6)} %compare.5), kind=kLoop, calls=%fused_computation.59.clone.1 | loop fusion | flops 4194304 | bytes 25165824 | tf_op jit(solution)/shard_map/while/body/eval_jaxpr/add | solution.py:112
  202.9 4.3 conditional.3
  202.9 4.3 broadcast.78
  207.2 1.3 collective-permute-start
  208.5 11.2 %select_add_fusion.2 = f32[512,4096]{0,1:T(8,128)} fusion(f32[512,4096]{0,1:T(8,128)} %get-tuple-element.522, f32[512,4096]{0,1:T(8,128)} %get-tuple-element.545, pred[]{:T(512)S(6)} %compare.5), kind=kLoop, calls=%fused_computation.59.clone.1 | loop fusion | flops 4194304 | bytes 25165824 | tf_op jit(solution)/shard_map/while/body/eval_jaxpr/add | solution.py:112
  220.9 4.3 conditional.3
  220.9 4.3 broadcast.78
  225.2 1.3 collective-permute-start
  226.5 11.2 %select_add_fusion.2 = f32[512,4096]{0,1:T(8,128)} fusion(f32[512,4096]{0,1:T(8,128)} %get-tuple-element.522, f32[512,4096]{0,1:T(8,128)} %get-tuple-element.545, pred[]{:T(512)S(6)} %compare.5), kind=kLoop, calls=%fused_computation.59.clone.1 | loop fusion | flops 4194304 | bytes 25165824 | tf_op jit(solution)/shard_map/while/body/eval_jaxpr/add | solution.py:112
  238.9 4.3 conditional.3
  238.9 4.3 broadcast.78
  243.2 1.3 collective-permute-start
  244.5 11.2 %select_add_fusion.2 = f32[512,4096]{0,1:T(8,128)} fusion(f32[512,4096]{0,1:T(8,128)} %get-tuple-element.522, f32[512,4096]{0,1:T(8,128)} %get-tuple-element.545, pred[]{:T(512)S(6)} %compare.5), kind=kLoop, calls=%fused_computation.59.clone.1 | loop fusion | flops 4194304 | bytes 25165824 | tf_op jit(solution)/shard_map/while/body/eval_jaxpr/add | solution.py:112
  256.9 4.3 conditional.3
  256.9 4.3 broadcast.78
  262.5 11.2 %select_add_fusion.2 = f32[512,4096]{0,1:T(8,128)} fusion(f32[512,4096]{0,1:T(8,128)} %get-tuple-element.522, f32[512,4096]{0,1:T(8,128)} %get-tuple-element.545, pred[]{:T(512)S(6)} %compare.5), kind=kLoop, calls=%fused_computation.59.clone.1 | loop fusion | flops 4194304 | bytes 25165824 | tf_op jit(solution)/shard_map/while/body/eval_jaxpr/add | solution.py:112
  274.9 4.3 conditional.3
  274.9 4.3 broadcast.78
  280.5 11.2 %select_add_fusion.2 = f32[512,4096]{0,1:T(8,128)} fusion(f32[512,4096]{0,1:T(8,128)} %get-tuple-element.522, f32[512,4096]{0,1:T(8,128)} %get-tuple-element.545, pred[]{:T(512)S(6)} %compare.5), kind=kLoop, calls=%fused_computation.59.clone.1 | loop fusion | flops 4194304 | bytes 25165824 | tf_op jit(solution)/shard_map/while/body/eval_jaxpr/add | solution.py:112
  291.9 34.6 %collective-permute-done = bf16[1,512,512]{2,1,0:T(8,128)(2,1)S(1)} collective-permute-done((bf16[1,512,512]{2,1,0:T(8,128)(2,1)S(1)}, bf16[1,512,512]{2,1,0:T(8,128)(2,1)S(1)}, u32[]{:S(2)}, u32[]{:S(2)}) %collective-permute-start) | collective-permute-done | bytes 524320 | tf_op jit(solution)/shard_map/while/body/eval_jaxpr/ppermute | solution.py:10
  326.6 16.7 %conditional.3 = (bf16[1,512,512]{2,1,0:T(8,128)(2,1)S(1)}, f32[512,4096]{0,1:T(8,128)}) conditional(s32[]{:T(128)} %convert_element_type.39, () %tuple.71, (pred[]{:T(512)}, bf16[2,512,512]{2,1,0:T(8,128)(2,1)}, s32[]{:T(128)}, bf16[1,512,512]{2,1,0:T(8,128)(2,1)S(1)}, bf16[2,512,512]{2,1,0:T(8,128)(2,1)}, /*index=5*/bf16[512,1024]{1,0:T(8,128)(2,1)}, ...), branch_computations={%region_1.1_spmd, %region_2.6_spmd} | conditional | flops 5932583424 | bytes 80746224 | solution.py:111
  327.8 1.3 dynamic-slice_select_fusion
  330.2 1.8 convolution_bitcast_fusion.1
  334.1 1.8 convolution_bitcast_fusion
  337.3 1.8 fusion.12
  339.1 4.2 pad_maximum_fusion
  344.6 11.2 %select_add_fusion.2 = f32[512,4096]{0,1:T(8,128)} fusion(f32[512,4096]{0,1:T(8,128)} %get-tuple-element.522, f32[512,4096]{0,1:T(8,128)} %get-tuple-element.545, pred[]{:T(512)S(6)} %compare.5), kind=kLoop, calls=%fused_computation.59.clone.1 | loop fusion | flops 4194304 | bytes 25165824 | tf_op jit(solution)/shard_map/while/body/eval_jaxpr/add | solution.py:112
  356.0 1.6 collective-permute-done
  357.6 16.7 %conditional.3 = (bf16[1,512,512]{2,1,0:T(8,128)(2,1)S(1)}, f32[512,4096]{0,1:T(8,128)}) conditional(s32[]{:T(128)} %convert_element_type.39, () %tuple.71, (pred[]{:T(512)}, bf16[2,512,512]{2,1,0:T(8,128)(2,1)}, s32[]{:T(128)}, bf16[1,512,512]{2,1,0:T(8,128)(2,1)S(1)}, bf16[2,512,512]{2,1,0:T(8,128)(2,1)}, /*index=5*/bf16[512,1024]{1,0:T(8,128)(2,1)}, ...), branch_computations={%region_1.1_spmd, %region_2.6_spmd} | conditional | flops 5932583424 | bytes 80746224 | solution.py:111
  358.8 1.3 dynamic-slice_select_fusion
  361.2 1.8 convolution_bitcast_fusion.1
  365.1 1.8 convolution_bitcast_fusion
  368.3 1.8 fusion.12
  370.1 4.2 pad_maximum_fusion
  375.6 11.2 %select_add_fusion.2 = f32[512,4096]{0,1:T(8,128)} fusion(f32[512,4096]{0,1:T(8,128)} %get-tuple-element.522, f32[512,4096]{0,1:T(8,128)} %get-tuple-element.545, pred[]{:T(512)S(6)} %compare.5), kind=kLoop, calls=%fused_computation.59.clone.1 | loop fusion | flops 4194304 | bytes 25165824 | tf_op jit(solution)/shard_map/while/body/eval_jaxpr/add | solution.py:112
  388.0 8.9 %copy.15 = f32[512,4096]{1,0:T(8,128)} copy(f32[512,4096]{0,1:T(8,128)} %get-tuple-element.365) | data formatting | bytes 16777216 | tf_op jit(solution)/shard_map/while | solution.py:129
  396.9 227.0 %reduce-scatter.2.cloned.1.call-done = f32[16,4096]{1,0:T(8,128)} async-done(((f32[512,4096]{1,0:T(8,128)}), f32[16,4096]{1,0:T(8,128)}) %reduce-scatter.2.cloned.1.call-update) | async-done | bytes 262160 | tf_op jit(solution)/shard_map/reduce_scatter | solution.py:132
  625.8 1.5 slice_bitcast_fusion.3
  (101 shorter events, 29.5 us)
Async XLA Ops:
  7.2 81.6 %all-gather.3.cloned.1.call-start = ((), (), s32[]{:S(2)}) async-start(), calls=%async_computation.1 | async-start | bytes 1081344 | tf_op jit(solution)/shard_map/all_gather | solution.py:66
  7.9 160.3 %all-gather.5.cloned.1.call-start = ((), (), s32[]{:S(2)}) async-start(), calls=%async_computation.2 | async-start | bytes 3244032 | tf_op jit(solution)/shard_map/all_gather | solution.py:65
  8.6 615.3 %reduce-scatter.2.cloned.1.call-start = ((), (), s32[]{:S(2)}) async-start(), calls=%async_computation.3 | async-start | bytes 8650752 | tf_op jit(solution)/shard_map/reduce_scatter | solution.py:132
  173.6 10.3 %collective-permute-start = (bf16[1,512,512]{2,1,0:T(8,128)(2,1)S(1)}, bf16[1,512,512]{2,1,0:T(8,128)(2,1)S(1)}, u32[]{:S(2)}, u32[]{:S(2)}) collective-permute-start(bf16[1,512,512]{2,1,0:T(8,128)(2,1)S(1)} %get-tuple-element.521), channel_id=1, source_target_pairs={{32,0},{64,32},{96,64},{128,96},{160,128},{192,160},{224,192},{33,... | collective-permute-start | bytes 1572872 | tf_op jit(solution)/shard_map/while/body/eval_jaxpr/ppermute | solution.py:10
  174.9 8.8 %copy-start = (bf16[2,512,512]{2,1,0:T(8,128)(2,1)S(1)}, bf16[2,512,512]{2,1,0:T(8,128)(2,1)}, u32[]{:S(2)}) copy-start(bf16[2,512,512]{2,1,0:T(8,128)(2,1)} %get-tuple-element.544) | copy-start | bytes 3145732 | tf_op jit(solution)/shard_map/while
  183.9 1.0 copy-start.1
  189.2 12.7 %collective-permute-start = (bf16[1,512,512]{2,1,0:T(8,128)(2,1)S(1)}, bf16[1,512,512]{2,1,0:T(8,128)(2,1)S(1)}, u32[]{:S(2)}, u32[]{:S(2)}) collective-permute-start(bf16[1,512,512]{2,1,0:T(8,128)(2,1)S(1)} %get-tuple-element.521), channel_id=1, source_target_pairs={{32,0},{64,32},{96,64},{128,96},{160,128},{192,160},{224,192},{33,... | collective-permute-start | bytes 1572872 | tf_op jit(solution)/shard_map/while/body/eval_jaxpr/ppermute | solution.py:10
  190.5 11.2 %copy-start = (bf16[2,512,512]{2,1,0:T(8,128)(2,1)S(1)}, bf16[2,512,512]{2,1,0:T(8,128)(2,1)}, u32[]{:S(2)}) copy-start(bf16[2,512,512]{2,1,0:T(8,128)(2,1)} %get-tuple-element.544) | copy-start | bytes 3145732 | tf_op jit(solution)/shard_map/while
  201.9 1.0 copy-start.1
  207.2 12.7 %collective-permute-start = (bf16[1,512,512]{2,1,0:T(8,128)(2,1)S(1)}, bf16[1,512,512]{2,1,0:T(8,128)(2,1)S(1)}, u32[]{:S(2)}, u32[]{:S(2)}) collective-permute-start(bf16[1,512,512]{2,1,0:T(8,128)(2,1)S(1)} %get-tuple-element.521), channel_id=1, source_target_pairs={{32,0},{64,32},{96,64},{128,96},{160,128},{192,160},{224,192},{33,... | collective-permute-start | bytes 1572872 | tf_op jit(solution)/shard_map/while/body/eval_jaxpr/ppermute | solution.py:10
  208.5 11.2 %copy-start = (bf16[2,512,512]{2,1,0:T(8,128)(2,1)S(1)}, bf16[2,512,512]{2,1,0:T(8,128)(2,1)}, u32[]{:S(2)}) copy-start(bf16[2,512,512]{2,1,0:T(8,128)(2,1)} %get-tuple-element.544) | copy-start | bytes 3145732 | tf_op jit(solution)/shard_map/while
  219.9 1.0 copy-start.1
  225.2 12.7 %collective-permute-start = (bf16[1,512,512]{2,1,0:T(8,128)(2,1)S(1)}, bf16[1,512,512]{2,1,0:T(8,128)(2,1)S(1)}, u32[]{:S(2)}, u32[]{:S(2)}) collective-permute-start(bf16[1,512,512]{2,1,0:T(8,128)(2,1)S(1)} %get-tuple-element.521), channel_id=1, source_target_pairs={{32,0},{64,32},{96,64},{128,96},{160,128},{192,160},{224,192},{33,... | collective-permute-start | bytes 1572872 | tf_op jit(solution)/shard_map/while/body/eval_jaxpr/ppermute | solution.py:10
  226.5 11.2 %copy-start = (bf16[2,512,512]{2,1,0:T(8,128)(2,1)S(1)}, bf16[2,512,512]{2,1,0:T(8,128)(2,1)}, u32[]{:S(2)}) copy-start(bf16[2,512,512]{2,1,0:T(8,128)(2,1)} %get-tuple-element.544) | copy-start | bytes 3145732 | tf_op jit(solution)/shard_map/while
  237.9 1.0 copy-start.1
  243.2 12.7 %collective-permute-start = (bf16[1,512,512]{2,1,0:T(8,128)(2,1)S(1)}, bf16[1,512,512]{2,1,0:T(8,128)(2,1)S(1)}, u32[]{:S(2)}, u32[]{:S(2)}) collective-permute-start(bf16[1,512,512]{2,1,0:T(8,128)(2,1)S(1)} %get-tuple-element.521), channel_id=1, source_target_pairs={{32,0},{64,32},{96,64},{128,96},{160,128},{192,160},{224,192},{33,... | collective-permute-start | bytes 1572872 | tf_op jit(solution)/shard_map/while/body/eval_jaxpr/ppermute | solution.py:10
  244.5 11.2 %copy-start = (bf16[2,512,512]{2,1,0:T(8,128)(2,1)S(1)}, bf16[2,512,512]{2,1,0:T(8,128)(2,1)}, u32[]{:S(2)}) copy-start(bf16[2,512,512]{2,1,0:T(8,128)(2,1)} %get-tuple-element.544) | copy-start | bytes 3145732 | tf_op jit(solution)/shard_map/while
  255.9 1.0 copy-start.1
  261.2 12.7 %collective-permute-start = (bf16[1,512,512]{2,1,0:T(8,128)(2,1)S(1)}, bf16[1,512,512]{2,1,0:T(8,128)(2,1)S(1)}, u32[]{:S(2)}, u32[]{:S(2)}) collective-permute-start(bf16[1,512,512]{2,1,0:T(8,128)(2,1)S(1)} %get-tuple-element.521), channel_id=1, source_target_pairs={{32,0},{64,32},{96,64},{128,96},{160,128},{192,160},{224,192},{33,... | collective-permute-start | bytes 1572872 | tf_op jit(solution)/shard_map/while/body/eval_jaxpr/ppermute | solution.py:10
  262.5 11.2 %copy-start = (bf16[2,512,512]{2,1,0:T(8,128)(2,1)S(1)}, bf16[2,512,512]{2,1,0:T(8,128)(2,1)}, u32[]{:S(2)}) copy-start(bf16[2,512,512]{2,1,0:T(8,128)(2,1)} %get-tuple-element.544) | copy-start | bytes 3145732 | tf_op jit(solution)/shard_map/while
  273.9 1.0 copy-start.1
  279.2 47.3 %collective-permute-start = (bf16[1,512,512]{2,1,0:T(8,128)(2,1)S(1)}, bf16[1,512,512]{2,1,0:T(8,128)(2,1)S(1)}, u32[]{:S(2)}, u32[]{:S(2)}) collective-permute-start(bf16[1,512,512]{2,1,0:T(8,128)(2,1)S(1)} %get-tuple-element.521), channel_id=1, source_target_pairs={{32,0},{64,32},{96,64},{128,96},{160,128},{192,160},{224,192},{33,... | collective-permute-start | bytes 1572872 | tf_op jit(solution)/shard_map/while/body/eval_jaxpr/ppermute | solution.py:10
  280.5 11.2 %copy-start = (bf16[2,512,512]{2,1,0:T(8,128)(2,1)S(1)}, bf16[2,512,512]{2,1,0:T(8,128)(2,1)}, u32[]{:S(2)}) copy-start(bf16[2,512,512]{2,1,0:T(8,128)(2,1)} %get-tuple-element.544) | copy-start | bytes 3145732 | tf_op jit(solution)/shard_map/while
  291.9 34.6 %copy-start.1 = (bf16[2,512,512]{2,1,0:T(8,128)(2,1)}, bf16[2,512,512]{2,1,0:T(8,128)(2,1)S(1)}, u32[]{:S(2)}) copy-start(bf16[2,512,512]{2,1,0:T(8,128)(2,1)S(1)} %select_dynamic-update-slice_fusion.2) | copy-start | bytes 3145732 | tf_op jit(solution)/shard_map/while
  326.6 3.6 copy-start.2
  330.2 1.9 copy-start.3
  343.3 14.3 %collective-permute-start = (bf16[1,512,512]{2,1,0:T(8,128)(2,1)S(1)}, bf16[1,512,512]{2,1,0:T(8,128)(2,1)S(1)}, u32[]{:S(2)}, u32[]{:S(2)}) collective-permute-start(bf16[1,512,512]{2,1,0:T(8,128)(2,1)S(1)} %get-tuple-element.521), channel_id=1, source_target_pairs={{32,0},{64,32},{96,64},{128,96},{160,128},{192,160},{224,192},{33,... | collective-permute-start | bytes 1572872 | tf_op jit(solution)/shard_map/while/body/eval_jaxpr/ppermute | solution.py:10
  344.6 11.2 %copy-start = (bf16[2,512,512]{2,1,0:T(8,128)(2,1)S(1)}, bf16[2,512,512]{2,1,0:T(8,128)(2,1)}, u32[]{:S(2)}) copy-start(bf16[2,512,512]{2,1,0:T(8,128)(2,1)} %get-tuple-element.544) | copy-start | bytes 3145732 | tf_op jit(solution)/shard_map/while
  356.0 1.6 copy-start.1
  357.6 3.6 copy-start.2
  361.2 1.9 copy-start.3
  374.3 12.7 %collective-permute-start = (bf16[1,512,512]{2,1,0:T(8,128)(2,1)S(1)}, bf16[1,512,512]{2,1,0:T(8,128)(2,1)S(1)}, u32[]{:S(2)}, u32[]{:S(2)}) collective-permute-start(bf16[1,512,512]{2,1,0:T(8,128)(2,1)S(1)} %get-tuple-element.521), channel_id=1, source_target_pairs={{32,0},{64,32},{96,64},{128,96},{160,128},{192,160},{224,192},{33,... | collective-permute-start | bytes 1572872 | tf_op jit(solution)/shard_map/while/body/eval_jaxpr/ppermute | solution.py:10
  375.6 11.2 %copy-start = (bf16[2,512,512]{2,1,0:T(8,128)(2,1)S(1)}, bf16[2,512,512]{2,1,0:T(8,128)(2,1)}, u32[]{:S(2)}) copy-start(bf16[2,512,512]{2,1,0:T(8,128)(2,1)} %get-tuple-element.544) | copy-start | bytes 3145732 | tf_op jit(solution)/shard_map/while
  387.0 1.0 copy-start.1
Sparse Core Ops, SparseCore 0:
  10.6 78.1 all-gather.2
  91.3 76.7 all-gather.4
  397.0 226.8 reduce-scatter.1
where the time goes:
time: 635 us; the launch traced here: 634 us
  waiting for transfers between devices  424 us (67%)
  other arithmetic  115 us (18%)
  local copies, waits for them, and re-layouts  53.3 us (8%)
  matrix products  14.9 us (2%)
  between operations  13.8 us (2%)
  starting transfers between devices  11.6 us (2%)
    reduce_scatter x1, waiting for transfers between devices, local(): shares = lax.psum_scatter(grad_acc, 'dp', scatter_dimension=0, tiled=True)  227 us
    add x9, other arithmetic, step_fn(): grad_acc = grad_acc + grad_term  98.4 us
    all_gather x1, waiting for transfers between devices, local(): lax.all_gather(w_mix, 'dp', axis=1, tiled=True)  80 us
    all_gather x1, waiting for transfers between devices, local(): lax.all_gather(w_conv, 'dp', axis=1, tiled=True)  79.4 us
    ppermute x9, waiting for transfers between devices, passed_along(): lax.ppermute(value, axis, [(source, source + steps) for source in range(l...  36.2 us
    another operation x15, local copies, waits for them, and re-layouts  30.4 us
  transfers between devices with their start and end apart: 12, of which 5 were waited for; matrix products, arithmetic and copies ran while one was open for 16% of the time, Pallas kernels for 0%

commit v1 on v0

v1 whole, which is shorter than its diff:
```python
import functools
import heapq

import jax
import jax.numpy as jnp
from jax import lax
from jax.experimental import pallas as pl
from jax.experimental.pallas import tpu as pltpu
from jax.sharding import PartitionSpec as P

NZ, NY = 8, 4
UNIT = 128


def halves(piece):
    start, count = piece
    first = (count // UNIT + 1) // 2 * UNIT
    return (start, first), (start + first, count - first)


def wrap(offset, count):
    return (offset + count // 2 - 1) % count - (count // 2 - 1)


def gather_plan(split, width, rows, rate, lag):
    sizes = {"z": NZ, "y": NY}
    free, events, sends, order = {}, [], [], []
    seq = 0

    def send(now, group, axis, way, offset, piece):
        nonlocal seq
        if piece[1] == 0:
            return
        key = (axis, way)
        begin = max(now, free.get(key, 0.0))
        free[key] = begin + rows * piece[1] * 2 / rate
        ident = len(sends)
        shift = dict(offset)
        shift[axis] = wrap(shift[axis] - way, sizes[axis])
        sends.append((axis, way, dict(offset), shift, piece))
        order.append(("send", ident))
        heapq.heappush(events, (free[key] + lag, ident, group))
        seq += 1

    axes = (("z", "y"), ("y", "z"))
    pieces = ((0, split), (split, width - split))
    here = {"z": 0, "y": 0}
    for group in (0, 1):
        for way in (1, -1):
            send(0.0, group, axes[group][0], way, here, pieces[group])
    for group in (0, 1):
        for way in (1, -1):
            send(0.0, group, axes[group][1], way, here, pieces[group])
    last = 0.0
    while events:
        now, ident, group = heapq.heappop(events)
        last = now
        axis, way, _, offset, piece = sends[ident]
        order.append(("wait", ident))
        reach = sizes[axis] // 2
        done = abs(offset[axis]) if offset[axis] != reach else reach
        if done < reach - 1:
            send(now, group, axis, way, offset, piece)
        elif done == reach - 1:
            send(now, group, axis, way, offset, halves(piece)[0 if way > 0 else 1])
        if axis == axes[group][0]:
            for side in (1, -1):
                send(now, group, axes[group][1], side, offset, piece)
    return sends, order, last


def scatter_plan(split, width, rows, rate, lag, cost):
    sizes = {"z": NZ, "y": NY}
    axes = (("z", "y"), ("y", "z"))
    pieces = ((0, split), (split, width - split))
    tasks = {}
    for group in (0, 1):
        one, two = axes[group]
        h1, h2 = sizes[one] // 2, sizes[two] // 2
        part1 = halves(pieces[group])
        others = [h2] + [s * j for j in range(h2 - 1, 0, -1) for s in (1, -1)] + [0]
        for rank, o2 in enumerate(others):
            for way in (1, -1):
                for j in range(h1, 0, -1):
                    piece = pieces[group] if j < h1 else part1[0 if way > 0 else 1]
                    needs = [(group, 1, way, j + 1, o2)] if j < h1 else []
                    tasks[(group, 1, way, j, o2)] = dict(
                        axis=one, way=way, block={one: way * j, two: o2}, piece=piece,
                        recvs=needs, locals=[], rank=(rank, -j))
            tasks[(group, 1, 0, 0, o2)] = dict(
                axis=None, way=0, block={one: 0, two: o2}, piece=pieces[group],
                recvs=[(group, 1, 1, 1, o2), (group, 1, -1, 1, o2)], locals=[], rank=(rank, 0))
        for way in (1, -1):
            for j in range(h2, 0, -1):
                piece = pieces[group] if j < h2 else part1[0 if way > 0 else 1]
                needs = [(group, 2, way, j + 1, 0)] if j < h2 else []
                at = way * j if j < h2 else h2
                tasks[(group, 2, way, j, 0)] = dict(
                    axis=two, way=way, block={one: 0, two: at}, piece=piece,
                    recvs=needs, locals=[(group, 1, 0, 0, at)], rank=(-1, -j))
        tasks[(group, 2, 0, 0, 0)] = dict(
            axis=None, way=0, block={one: 0, two: 0}, piece=pieces[group],
            recvs=[(group, 2, 1, 1, 0), (group, 2, -1, 1, 0)], locals=[(group, 1, 0, 0, 0)], rank=(-1, 0))
    arrive, finished, free, order, clock = {}, {}, {}, [], 0.0
    left = dict(tasks)
    while left:
        best = None
        for key, task in left.items():
            if any(n not in arrive for n in task["recvs"]) or any(n not in finished for n in task["locals"]):
                continue
            ready = max([clock] + [arrive[n] for n in task["recvs"]] + [finished[n] for n in task["locals"]])
            link = free.get((task["axis"], task["way"]), 0.0) if task["axis"] else 0.0
            score = (ready, task["rank"], link, key)
            if best is None or score < best[0]:
                best = (score, key, ready)
        _, key, ready = best
        task = left.pop(key)
        clock = ready + cost * rows * task["piece"][1]
        finished[key] = clock
        if task["axis"]:
            lane = (task["axis"], task["way"])
            begin = max(clock, free.get(lane, 0.0))
            free[lane] = begin + rows * task["piece"][1] * 2 / rate
            arrive[key] = free[lane] + lag
        order.append(key)
    return tasks, order, clock


F32, BF16 = jnp.float32, jnp.bfloat16
MESH = pl.DeviceIdType.MESH
SECTIONS = 8
C = 512
LEN = 512
ROWS = 1024
SHARD = 16
WIDTH = 4096
CONV = 3072
RES = slice(3072, 3584)
SKIP = slice(3584, 4096)
CHUNK = 256
CHUNKS = ROWS // CHUNK
PER_SEQ = LEN // CHUNK
PAD = 264
STRIDE = LEN + PAD
RATE, LAG = 46.5e3, 1.8
AG_SPLIT, RS_SPLIT = 2560, 1536
NT = (((1,), (1,)), ((), ()))


def dot(a, b):
    return jnp.dot(a, b, preferred_element_type=F32)


def dot_nt(a, b):
    return lax.dot_general(a, b, NT, preferred_element_type=F32)


def kernel(gather, scatter, slots, x_hbm, top_hbm, skip_hbm, w_hbm, cot_hbm, grad_hbm,
           w_v, x_v, xf_v, xt_v, ht_v, a1_v, a2_v, hs_v, pf_v, a_v, out_v, g_v,
           ra_v, rb_v, sa_v, sb_v,
           ag_send, ag_recv, rs_send, rs_recv, ch_send, ch_recv, ld_sem, st_sem):
    p = lax.axis_index("pipe")
    dp = lax.axis_index("dp")
    z, y = dp // NY, lax.rem(dp, NY)

    def dp_at(dz, dy):
        return lax.rem(z + (dz + NZ), NZ) * NY + lax.rem(y + (dy + NY), NY)

    def rows_at(offset):
        return pl.ds(pl.multiple_of(dp_at(offset["z"], offset["y"]) * SHARD, SHARD), SHARD)

    def peer(axis, way):
        return {"dp": dp_at(way, 0) if axis == "z" else dp_at(0, way)}

    is_last, is_first = p == SECTIONS - 1, p == 0

    x_load = pltpu.make_async_copy(x_hbm, x_v, ld_sem.at[0])
    skip_load = pltpu.make_async_copy(skip_hbm, a_v.at[:, SKIP], ld_sem.at[1])
    top_load = pltpu.make_async_copy(top_hbm, a_v.at[:, RES], ld_sem.at[2])
    own_load = pltpu.make_async_copy(w_hbm, w_v.at[rows_at({"z": 0, "y": 0}), :], ld_sem.at[3])
    x_load.start()
    skip_load.start()
    own_load.start()

    @pl.when(is_last)
    def _():
        top_load.start()

    barrier = pltpu.get_barrier_semaphore()
    for axis in ("z", "y"):
        for way in (1, -1):
            pl.semaphore_signal(barrier, inc=1, device_id=peer(axis, way), device_id_type=MESH)

    for way in (1, SECTIONS - 1):
        neighbour = {"pipe": lax.rem(p + way, SECTIONS)}
        pl.semaphore_signal(barrier, inc=1, device_id=neighbour, device_id_type=MESH)
    pl.semaphore_wait(barrier, 6)

    ag_sends, ag_order, _ = gather

    def ag_send_copy(ident):
        axis, way, offset, _, piece = ag_sends[ident]
        lanes = slice(piece[0], piece[0] + piece[1])
        here = w_v.at[rows_at(offset), lanes]
        own = offset["z"] == 0 and offset["y"] == 0
        source = w_hbm.at[:, lanes] if own else here
        return pltpu.make_async_remote_copy(
            source, here, ag_send.at[ident], ag_recv.at[ident],
            device_id=peer(axis, way), device_id_type=MESH)

    def ag_recv_copy(ident):
        axis, way, _, landed, piece = ag_sends[ident]
        lanes = slice(piece[0], piece[0] + piece[1])
        there = w_v.at[rows_at(landed), lanes]
        return pltpu.make_async_remote_copy(
            there, there, ag_send.at[ident], ag_recv.at[ident],
            device_id=peer(axis, -way), device_id_type=MESH)

    started = False
    for what, ident in ag_order:
        if what == "send":
            ag_send_copy(ident).start()
            continue
        if not started:
            started = True
            x_load.wait()
            for s in range(2):
                xf_v[s * STRIDE:s * STRIDE + PAD, :] = jnp.zeros((PAD, C), F32)
                xf_v[s * STRIDE + PAD:(s + 1) * STRIDE, :] = x_v[s * LEN:(s + 1) * LEN, :].astype(F32)
                pf_v[s * STRIDE + LEN:(s + 1) * STRIDE, :] = jnp.zeros((PAD, 2 * C), F32)
        ag_recv_copy(ident).wait_recv()
    own_load.wait()
    skip_load.wait()

    d = (1 + lax.rem(p, 2)) * (1 + 3 * lax.rem(p // 2, 2)) * (1 + 15 * (p // 4))

    def shifted(ref, base, shift_down, shift):
        window = ref[pl.ds(pl.multiple_of(base, 8), CHUNK + 8), :]
        return pltpu.roll(window, shift_down, 0)[8:8 + CHUNK].astype(BF16)

    def delayed(s, t, shift):
        down = lax.rem(shift, 8)
        return shifted(xf_v, s * STRIDE + PAD + t - (shift - down) - 8, down, shift)

    def advanced(s, t, shift):
        down = lax.rem(8 - lax.rem(shift, 8), 8)
        return shifted(pf_v, s * STRIDE + t + (shift + down) - 8, down, shift)

    def place(q):
        s = q // PER_SEQ
        t = (PER_SEQ - 1 - lax.rem(q, PER_SEQ)) * CHUNK
        row = pl.multiple_of(s * LEN + t, CHUNK)
        return s, t, pl.ds(row, CHUNK)

    def forward(q):
        s, t, rows = place(q)
        x0 = x_v[rows, :]
        pre = dot(x0, w_v[:, 0:1024])
        pre = pre + dot(delayed(s, t, d), w_v[:, 1024:2048])
        pre = pre + dot(delayed(s, t, 2 * d), w_v[:, 2048:3072])
        filt = jnp.tanh(pre[:, :C])
        gate = jax.nn.sigmoid(pre[:, C:])
        a1_v[rows, :] = gate * (1.0 - filt * filt)
        hid = filt * gate
        a2_v[rows, :] = hid * (1.0 - gate)
        ht_v[:, rows] = hid.astype(BF16).T
        xt_v[:, rows] = x0.T
        hs_v[rows, :] = dot_nt(a_v[rows, SKIP], w_v[:, SKIP])

    def forward_step(q, carry):
        forward(q)
        return carry

    lax.fori_loop(0, jnp.where(is_last, 1, CHUNKS), forward_step, 0)

    @pl.when(is_last)
    def _():
        top_load.wait()

    def chain_send(q):
        _, _, rows = place(q)
        return pltpu.make_async_remote_copy(
            out_v.at[rows, :], a_v.at[rows, RES], ch_send.at[q], ch_recv.at[q],
            device_id={"pipe": p - 1}, device_id_type=MESH)

    def chain_recv(q):
        _, _, rows = place(q)
        return pltpu.make_async_remote_copy(
            a_v.at[rows, RES], a_v.at[rows, RES], ch_send.at[q], ch_recv.at[q],
            device_id={"pipe": p + 1}, device_id_type=MESH)

    def chain_store(q):
        _, _, rows = place(q)
        return pltpu.make_async_copy(out_v.at[rows, :], cot_hbm.at[rows, :], st_sem.at[q])

    def chain_step(q, carry):
        s, t, rows = place(q)

        @pl.when(jnp.logical_not(is_last))
        def _():
            chain_recv(q).wait_recv()

        g = a_v[rows, RES]
        hg = hs_v[rows, :] + dot_nt(g, w_v[:, RES])
        pg1 = (hg * a1_v[rows, :]).astype(BF16)
        pg2 = (hg * a2_v[rows, :]).astype(BF16)
        a_v[rows, 0:C] = pg1
        a_v[rows, C:2 * C] = pg2
        prow = pl.ds(pl.multiple_of(s * STRIDE + t, 8), CHUNK)
        pf_v[prow, 0:C] = pg1.astype(F32)
        pf_v[prow, C:2 * C] = pg2.astype(F32)
        a_v[rows, 1024:2048] = advanced(s, t, d)
        a_v[rows, 2048:3072] = advanced(s, t, 2 * d)
        out = g.astype(F32) + dot_nt(a_v[rows, 0:CONV], w_v[:, 0:CONV])
        out_v[rows, :] = out.astype(BF16)

        @pl.when(jnp.logical_not(is_first))
        def _():
            chain_send(q).start()

        chain_store(q).start()

        @pl.when(jnp.logical_and(is_last, q < CHUNKS - 1))
        def _():
            forward(jnp.minimum(q + 1, CHUNKS - 1))

        return carry

    lax.fori_loop(0, CHUNKS, chain_step, 0)

    def grad_step(lhs_v, n, carry):
        lanes = pl.ds(pl.multiple_of(n * C, C), C)
        g_v[:, lanes] = dot(lhs_v[...], a_v[:, lanes])
        return carry

    lax.fori_loop(0, 6, functools.partial(grad_step, xt_v), 0)
    lax.fori_loop(6, 8, functools.partial(grad_step, ht_v), 0)

    rs_tasks, rs_order, _ = scatter
    starts = (0, RS_SPLIT)
    recv_bufs, send_bufs = (ra_v, rb_v), (sa_v, sb_v)

    def rs_copy(key):
        task = rs_tasks[key]
        group, slot, sem = slots[key]
        lo = task["piece"][0] - starts[group]
        lanes = slice(lo, lo + task["piece"][1])
        source = send_bufs[group].at[slot, :, lanes]
        target = recv_bufs[group].at[slot, :, lanes]
        return pltpu.make_async_remote_copy(
            source, target, rs_send.at[sem], rs_recv.at[sem],
            device_id=peer(task["axis"], task["way"]), device_id_type=MESH)

    def rs_take(key):
        task = rs_tasks[key]
        group, slot, sem = slots[key]
        lo = task["piece"][0] - starts[group]
        view = recv_bufs[group].at[slot, :, lo:lo + task["piece"][1]]
        pltpu.make_async_remote_copy(
            view, view, rs_send.at[sem], rs_recv.at[sem],
            device_id=peer(task["axis"], -task["way"]), device_id_type=MESH).wait_recv()
        return group, slot, task["piece"]

    for key in rs_order:
        task = rs_tasks[key]
        rows = rows_at({"z": task["block"]["z"], "y": task["block"]["y"]})
        first, count = task["piece"]
        got = [rs_take(need) for need in task["recvs"]]
        if task["axis"] is None:
            total = g_v[rows, first:first + count]
            for group, slot, piece in got:
                total = total + recv_bufs[group][slot, :, 0:count].astype(F32)
            g_v[rows, first:first + count] = total
            continue
        group, slot, _ = slots[key]
        base = starts[group]
        spans = [(first, count, None)]
        if got:
            _, have, (p0, pn) = got[0]
            spans = [(p0, pn, have)]
            if p0 > first:
                spans.append((first, p0 - first, None))
            if p0 + pn < first + count:
                spans.append((p0 + pn, first + count - p0 - pn, None))
        for lo, n, have in spans:
            value = g_v[rows, lo:lo + n]
            if have is not None:
                value = value + recv_bufs[group][have, :, lo - base:lo - base + n].astype(F32)
            send_bufs[group][slot, :, lo - base:lo - base + n] = value.astype(BF16)
        rs_copy(key).start()

    grad_store = pltpu.make_async_copy(g_v.at[rows_at({"z": 0, "y": 0}), :], grad_hbm, ld_sem.at[0])
    grad_store.start()

    for ident in range(len(ag_sends)):
        ag_send_copy(ident).wait_send()
    for key in rs_order:
        if rs_tasks[key]["axis"] is not None:
            rs_copy(key).wait_send()
    for q in range(CHUNKS):
        chain_store(q).wait()

        @pl.when(jnp.logical_not(is_first))
        def _():
            chain_send(q).wait_send()

    grad_store.wait()


def local(x_ckpt, top_cot, skip_cot, w_conv, w_mix):
    x = x_ckpt.reshape(ROWS, C)
    top = top_cot.reshape(ROWS, C)
    skip = skip_cot.reshape(ROWS, C)
    w = jnp.concatenate([w_conv.reshape(SHARD, CONV), w_mix.reshape(SHARD, 2 * C)], axis=1)
    gather = gather_plan(AG_SPLIT, WIDTH, SHARD, RATE, LAG)
    scatter = scatter_plan(RS_SPLIT, WIDTH, SHARD, RATE, LAG, 2e-6)
    slots, counts, sems = {}, [0, 0], 0
    for key, task in scatter[0].items():
        if task["axis"] is not None:
            slots[key] = (key[0], counts[key[0]], sems)
            counts[key[0]] += 1
            sems += 1
    sends = len(gather[0])
    anywhere = pl.BlockSpec(memory_space=pl.ANY)
    dma = pltpu.SemaphoreType.DMA
    cot, grad = pl.pallas_call(
        functools.partial(kernel, gather, scatter, slots),
        out_shape=(
            jax.ShapeDtypeStruct((ROWS, C), BF16),
            jax.ShapeDtypeStruct((SHARD, WIDTH), F32),
        ),
        in_specs=[anywhere] * 4,
        out_specs=(anywhere, anywhere),
        scratch_shapes=[
            pltpu.VMEM((C, WIDTH), BF16),
            pltpu.VMEM((ROWS, C), BF16),
            pltpu.VMEM((2 * STRIDE, C), F32),
            pltpu.VMEM((C, ROWS), BF16),
            pltpu.VMEM((C, ROWS), BF16),
            pltpu.VMEM((ROWS, C), F32),
            pltpu.VMEM((ROWS, C), F32),
            pltpu.VMEM((ROWS, C), F32),
            pltpu.VMEM((2 * STRIDE, 2 * C), F32),
            pltpu.VMEM((ROWS, WIDTH), BF16),
            pltpu.VMEM((ROWS, C), BF16),
            pltpu.VMEM((C, WIDTH), F32),
            pltpu.VMEM((counts[0], SHARD, RS_SPLIT), BF16),
            pltpu.VMEM((counts[1], SHARD, WIDTH - RS_SPLIT), BF16),
            pltpu.VMEM((counts[0], SHARD, RS_SPLIT), BF16),
            pltpu.VMEM((counts[1], SHARD, WIDTH - RS_SPLIT), BF16),
            dma((sends,)), dma((sends,)), dma((sems,)), dma((sems,)),
            dma((CHUNKS,)), dma((CHUNKS,)), dma((4,)), dma((CHUNKS,)),
        ],
        compiler_params=pltpu.CompilerParams(
            collective_id=0, has_side_effects=True, vmem_limit_bytes=67043328),
    )(x, top, skip, w)
    return (
        cot.reshape(x_ckpt.shape),
        grad[:, :CONV].reshape(w_conv.shape),
        grad[:, CONV:].reshape(w_mix.shape),
    )


def solution(mesh):
    placed = (
        P("pipe", None, "dp", None, None),
        P(None, "dp", None, None),
        P(None, "dp", None, None),
        P("pipe", "dp", None, None),
        P("pipe", "dp", None),
    )
    return jax.shard_map(
        local,
        mesh=mesh,
        in_specs=placed,
        out_specs=(
            P("pipe", None, "dp", None, None),
            P("pipe", "dp", None, None),
            P("pipe", "dp", None),
        ),
        check_vma=False,
    )
```

time: 635 us -> 127 us (0.20)
  waiting for transfers between devices: 424 us -> 0 us
  Pallas kernels: 0 us -> 119 us
  other arithmetic: 115 us -> 0.66 us
  local copies, waits for them, and re-layouts: 53.3 us -> 6.14 us
  matrix products: 14.9 us -> 0 us
  between operations: 13.8 us -> 0.68 us
  starting transfers between devices: 11.6 us -> 0 us
    reduce_scatter x1 -> x0, waiting for transfers between devices: 227 us -> none  [local(): shares = lax.psum_scatter(grad_acc, 'dp', scatter_dimension=0, tiled=True)]
    all_gather x2 -> x0, waiting for transfers between devices: 159 us -> none  [the longest x1 80 us: local(): lax.all_gather(w_mix, 'dp', axis=1, tiled=True)]
    pallas_call x0 -> x1, Pallas kernels: none -> 119 us  [local(): pl.pallas_call(functools.partial(kernel, gather, scatter, slots), out_sha...]
    add x9 -> x0, other arithmetic: 98.4 us -> none  [step_fn(): grad_acc = grad_acc + grad_term]
    ppermute x9 -> x0, waiting for transfers between devices: 36.2 us -> none  [passed_along(): lax.ppermute(value, axis, [(source, source + steps) for source in range(l...]
    another operation x16 -> x0, local copies, waits for them, and re-layouts: 30.6 us -> none
    while x37 -> x0, local copies, waits for them, and re-layouts: 15.7 us -> none  [the longest x1 8.92 us: local(): final_state = lax.fori_loop(0, step_count, step_fn, initial)]
    dot_general x10 -> x0, matrix products: 14.9 us -> none  [the longest x2 3.69 us: layer_back(): jnp.einsum('slkc,ckn->sln', tapped_x, conv_w, preferred_element_type=jnp....]
  transfers between devices with their start and end apart: 12 -> 0, of which waited for: 5 -> 0; matrix products, arithmetic and copies ran while one was open for 16% -> 0% of each run, Pallas kernels for 0% -> 0%
where the time goes in v1:
time: 127 us
  Pallas kernels  119 us (94%)
  local copies, waits for them, and re-layouts  6.14 us (5%)
    pallas_call x1, Pallas kernels, local(): pl.pallas_call(functools.partial(kernel, gather, scatter, slots), out_sha...  119 us
    unnamed x8, local copies, waits for them, and re-layouts  3.5 us

profile of v1, /device:TPU:8, one launch (start us, length us, event | category | flops | bytes accessed | tf_op | source)
XLA Modules:
  0.0 126.5 jit_solution(17338793741126281016)
XLA Ops:
  0.6 1.0 copy.11
  1.6 0.0 copy-start.1
  1.7 0.7 copy-done.1
  2.4 0.7 pad_maximum_fusion.w_hbm
  3.0 119.0 %shard_map.76 = (bf16[1024,512]{1,0:T(8,128)(2,1)}, f32[16,4096]{1,0:T(8,128)}) custom-call(bf16[1024,512]{1,0:T(8,128)(2,1)} %bitcast.12, bf16[1024,512]{1,0:T(8,128)(2,1)} %bitcast.13, bf16[1024,512]{1,0:T(8,128)(2,1)} %bitcast.14, bf16[16,4096]{1,0:T(8,128)(2,1)} %pad_maximum_fusion.w_hbm), custom_call_target="tpu_custom_call" | custom-call | tf_op jit(solution)/shard_map/pallas_call | solution.py:426
  122.1 0.0 copy-start
  122.1 1.6 %slice_bitcast_fusion = f32[1,16,1024]{2,1,0:T(8,128)} fusion(f32[16,4096]{1,0:T(8,128)} %get-tuple-element.6), kind=kLoop, calls=%fused_computation.1 | loop fusion | bytes 131072 | tf_op jit(solution)/shard_map/reshape | solution.py:460
  123.6 0.9 slice.6
  124.6 0.1 reshape.36
  124.7 0.8 copy.13
  125.5 0.0 copy-done
  125.5 1.0 copy.16
  (1 shorter events, 0.0 us)
Async XLA Ops:
  1.6 0.8 copy-start.1
  122.1 3.5 %copy-start = (bf16[1024,512]{1,0:T(8,128)(2,1)S(1)}, bf16[1024,512]{1,0:T(8,128)(2,1)}, u32[]{:S(2)}) copy-start(bf16[1024,512]{1,0:T(8,128)(2,1)} %get-tuple-element.5) | copy-start | bytes 3145732

commit v2 on v1

--- a/solution.py
+++ b/solution.py
@@ -155,8 +155,8 @@
     return lax.dot_general(a, b, NT, preferred_element_type=F32)
 
 
-def kernel(gather, scatter, slots, x_hbm, top_hbm, skip_hbm, w_hbm, cot_hbm, grad_hbm,
-           w_v, x_v, xf_v, xt_v, ht_v, a1_v, a2_v, hs_v, pf_v, a_v, out_v, g_v,
+def kernel(gather, scatter, slots, x_hbm, top_hbm, skip_hbm, wc_hbm, wm_hbm, cot_hbm, conv_hbm, mix_hbm,
+           wc_v, w_v, x_v, xf_v, xt_v, ht_v, a1_v, a2_v, hs_v, pf_v, a_v, out_v, g_v,
            ra_v, rb_v, sa_v, sb_v,
            ag_send, ag_recv, rs_send, rs_recv, ch_send, ch_recv, ld_sem, st_sem):
     p = lax.axis_index("pipe")
@@ -177,10 +177,13 @@
     x_load = pltpu.make_async_copy(x_hbm, x_v, ld_sem.at[0])
     skip_load = pltpu.make_async_copy(skip_hbm, a_v.at[:, SKIP], ld_sem.at[1])
     top_load = pltpu.make_async_copy(top_hbm, a_v.at[:, RES], ld_sem.at[2])
-    own_load = pltpu.make_async_copy(w_hbm, w_v.at[rows_at({"z": 0, "y": 0}), :], ld_sem.at[3])
+    own = rows_at({"z": 0, "y": 0})
+    wc_load = pltpu.make_async_copy(wc_hbm, wc_v, ld_sem.at[3])
+    wm_load = pltpu.make_async_copy(wm_hbm, w_v.at[own, CONV:WIDTH], ld_sem.at[4])
+    wc_load.start()
+    wm_load.start()
     x_load.start()
     skip_load.start()
-    own_load.start()
 
     @pl.when(is_last)
     def _():
@@ -194,6 +197,11 @@
     for way in (1, SECTIONS - 1):
         neighbour = {"pipe": lax.rem(p + way, SECTIONS)}
         pl.semaphore_signal(barrier, inc=1, device_id=neighbour, device_id_type=MESH)
+    wc_load.wait()
+    taps = wc_v[...].astype(F32)
+    for k in range(3):
+        w_v[own, k * 1024:(k + 1) * 1024] = taps[:, k, :].astype(BF16)
+    wm_load.wait()
     pl.semaphore_wait(barrier, 6)
 
     ag_sends, ag_order, _ = gather
@@ -202,10 +210,8 @@
         axis, way, offset, _, piece = ag_sends[ident]
         lanes = slice(piece[0], piece[0] + piece[1])
         here = w_v.at[rows_at(offset), lanes]
-        own = offset["z"] == 0 and offset["y"] == 0
-        source = w_hbm.at[:, lanes] if own else here
         return pltpu.make_async_remote_copy(
-            source, here, ag_send.at[ident], ag_recv.at[ident],
+            here, here, ag_send.at[ident], ag_recv.at[ident],
             device_id=peer(axis, way), device_id_type=MESH)
 
     def ag_recv_copy(ident):
@@ -229,22 +235,24 @@
                 xf_v[s * STRIDE + PAD:(s + 1) * STRIDE, :] = x_v[s * LEN:(s + 1) * LEN, :].astype(F32)
                 pf_v[s * STRIDE + LEN:(s + 1) * STRIDE, :] = jnp.zeros((PAD, 2 * C), F32)
         ag_recv_copy(ident).wait_recv()
-    own_load.wait()
     skip_load.wait()
 
     d = (1 + lax.rem(p, 2)) * (1 + 3 * lax.rem(p // 2, 2)) * (1 + 15 * (p // 4))
 
-    def shifted(ref, base, shift_down, shift):
+    def shifted(ref, base, down):
         window = ref[pl.ds(pl.multiple_of(base, 8), CHUNK + 8), :]
-        return pltpu.roll(window, shift_down, 0)[8:8 + CHUNK].astype(BF16)
+        width = window.shape[1]
+        turned = pltpu.roll(window.reshape(CHUNK // 8 + 1, 8, width), down, 1)
+        inner = lax.broadcasted_iota(jnp.int32, (CHUNK // 8, 8, width), 1) >= down
+        return jnp.where(inner, turned[1:], turned[:-1]).reshape(CHUNK, width).astype(BF16)
 
     def delayed(s, t, shift):
         down = lax.rem(shift, 8)
-        return shifted(xf_v, s * STRIDE + PAD + t - (shift - down) - 8, down, shift)
+        return shifted(xf_v, s * STRIDE + PAD + t - (shift - down) - 8, down)
 
     def advanced(s, t, shift):
         down = lax.rem(8 - lax.rem(shift, 8), 8)
-        return shifted(pf_v, s * STRIDE + t + (shift + down) - 8, down, shift)
+        return shifted(pf_v, s * STRIDE + t + (shift + down) - 8, down)
 
     def place(q):
         s = q // PER_SEQ
@@ -326,15 +334,31 @@
 
         return carry
 
-    lax.fori_loop(0, CHUNKS, chain_step, 0)
-
-    def grad_step(lhs_v, n, carry):
+    def grad_step(lhs_v, s, add, n, carry):
         lanes = pl.ds(pl.multiple_of(n * C, C), C)
-        g_v[:, lanes] = dot(lhs_v[...], a_v[:, lanes])
+        rows = slice(s * LEN, (s + 1) * LEN)
+        term = dot(lhs_v[:, rows], a_v[rows, lanes])
+        g_v[:, lanes] = g_v[:, lanes] + term if add else term
         return carry
 
-    lax.fori_loop(0, 6, functools.partial(grad_step, xt_v), 0)
-    lax.fori_loop(6, 8, functools.partial(grad_step, ht_v), 0)
+    def grads(s, add):
+        lax.fori_loop(0, 6, functools.partial(grad_step, xt_v, s, add), 0)
+        lax.fori_loop(6, 8, functools.partial(grad_step, ht_v, s, add), 0)
+
+    early = p < 2
+    lax.fori_loop(0, PER_SEQ, chain_step, 0)
+
+    @pl.when(early)
+    def _():
+        grads(0, False)
+
+    lax.fori_loop(PER_SEQ, CHUNKS, chain_step, 0)
+
+    @pl.when(jnp.logical_not(early))
+    def _():
+        grads(0, False)
+
+    grads(1, True)
 
     rs_tasks, rs_order, _ = scatter
     starts = (0, RS_SPLIT)
@@ -389,8 +413,14 @@
             send_bufs[group][slot, :, lo - base:lo - base + n] = value.astype(BF16)
         rs_copy(key).start()
 
-    grad_store = pltpu.make_async_copy(g_v.at[rows_at({"z": 0, "y": 0}), :], grad_hbm, ld_sem.at[0])
-    grad_store.start()
+    own_rows = rows_at({"z": 0, "y": 0})
+    grad_stores = [
+        pltpu.make_async_copy(
+            g_v.at[own_rows, k * 1024:(k + 1) * 1024], conv_hbm.at[k] if k < 3 else mix_hbm, ld_sem.at[k])
+        for k in range(4)
+    ]
+    for store in grad_stores:
+        store.start()
 
     for ident in range(len(ag_sends)):
         ag_send_copy(ident).wait_send()
@@ -404,14 +434,16 @@
         def _():
             chain_send(q).wait_send()
 
-    grad_store.wait()
+    for store in grad_stores:
+        store.wait()
 
 
 def local(x_ckpt, top_cot, skip_cot, w_conv, w_mix):
     x = x_ckpt.reshape(ROWS, C)
     top = top_cot.reshape(ROWS, C)
     skip = skip_cot.reshape(ROWS, C)
-    w = jnp.concatenate([w_conv.reshape(SHARD, CONV), w_mix.reshape(SHARD, 2 * C)], axis=1)
+    taps = w_conv.reshape(SHARD, 3, 2 * C)
+    mix = w_mix.reshape(SHARD, 2 * C)
     gather = gather_plan(AG_SPLIT, WIDTH, SHARD, RATE, LAG)
     scatter = scatter_plan(RS_SPLIT, WIDTH, SHARD, RATE, LAG, 2e-6)
     slots, counts, sems = {}, [0, 0], 0
@@ -423,15 +455,17 @@
     sends = len(gather[0])
     anywhere = pl.BlockSpec(memory_space=pl.ANY)
     dma = pltpu.SemaphoreType.DMA
-    cot, grad = pl.pallas_call(
+    cot, conv_grad, mix_grad = pl.pallas_call(
         functools.partial(kernel, gather, scatter, slots),
         out_shape=(
             jax.ShapeDtypeStruct((ROWS, C), BF16),
-            jax.ShapeDtypeStruct((SHARD, WIDTH), F32),
+            jax.ShapeDtypeStruct((3, SHARD, 2 * C), F32),
+            jax.ShapeDtypeStruct((SHARD, 2 * C), F32),
         ),
-        in_specs=[anywhere] * 4,
-        out_specs=(anywhere, anywhere),
+        in_specs=[anywhere] * 5,
+        out_specs=(anywhere,) * 3,
         scratch_shapes=[
+            pltpu.VMEM((SHARD, 3, 2 * C), BF16),
             pltpu.VMEM((C, WIDTH), BF16),
             pltpu.VMEM((ROWS, C), BF16),
             pltpu.VMEM((2 * STRIDE, C), F32),
@@ -449,15 +483,15 @@
             pltpu.VMEM((counts[0], SHARD, RS_SPLIT), BF16),
             pltpu.VMEM((counts[1], SHARD, WIDTH - RS_SPLIT), BF16),
             dma((sends,)), dma((sends,)), dma((sems,)), dma((sems,)),
-            dma((CHUNKS,)), dma((CHUNKS,)), dma((4,)), dma((CHUNKS,)),
+            dma((CHUNKS,)), dma((CHUNKS,)), dma((5,)), dma((CHUNKS,)),
         ],
         compiler_params=pltpu.CompilerParams(
             collective_id=0, has_side_effects=True, vmem_limit_bytes=67043328),
-    )(x, top, skip, w)
+    )(x, top, skip, taps, mix)
     return (
         cot.reshape(x_ckpt.shape),
-        grad[:, :CONV].reshape(w_conv.shape),
-        grad[:, CONV:].reshape(w_mix.shape),
+        conv_grad.transpose(1, 0, 2).reshape(w_conv.shape),
+        mix_grad.reshape(w_mix.shape),
     )
 
 

time: 127 us -> 122 us (0.961)
  Pallas kernels: 119 us -> 116 us
    pallas_call x1, Pallas kernels: 119 us -> 116 us  [local(): pl.pallas_call(functools.partial(kernel, gather, scatter, slots), out_sha...]
    unnamed x8, local copies, waits for them, and re-layouts: 3.5 us -> 5.43 us
    reshape x2 -> x0, local copies, waits for them, and re-layouts: 1.71 us -> none  [the longest x1 1.56 us: local(): grad[:, CONV:].reshape(w_mix.shape)]
where the time goes in v2:
time: 122 us
  Pallas kernels  116 us (95%)
  local copies, waits for them, and re-layouts  5.43 us (4%)
    pallas_call x1, Pallas kernels, local(): pl.pallas_call(functools.partial(kernel, gather, scatter, slots), out_sha...  116 us
    unnamed x8, local copies, waits for them, and re-layouts  5.43 us

profile of v2, /device:TPU:8, one launch (start us, length us, event | category | flops | bytes accessed | tf_op | source)
XLA Modules:
  0.0 121.7 jit_solution(5319315787373549535)
XLA Ops:
  0.6 1.6 %copy.11 = bf16[1,16,3,1024]{3,2,1,0:T(4,128)(2,1)} copy(bf16[1,16,3,1024]{3,1,2,0:T(8,128)(2,1)} %param.8) | data formatting | bytes 196608 | tf_op args[3]
  2.3 115.6 %shard_map.76 = (bf16[1024,512]{1,0:T(8,128)(2,1)}, f32[3,16,1024]{2,1,0:T(8,128)}, f32[16,1024]{1,0:T(8,128)}) custom-call(bf16[1024,512]{1,0:T(8,128)(2,1)} %bitcast.14, bf16[1024,512]{1,0:T(8,128)(2,1)} %bitcast.15, bf16[1024,512]{1,0:T(8,128)(2,1)} %bitcast.16, bf16[16,3,1024]{2,1,0:T(4,128)(2,1)} %bitcast.18, bf16[16,1024]{1,0:T(8,128)(2,1)} %bitcast.21), custom_call_target="tpu_custom_call" | custom-call | tf_op jit(solution)/shard_map/pallas_call | solution.py:458
  117.9 0.0 copy-start
  117.9 2.3 %copy.15 = bf16[1,2,1,512,512]{4,3,2,1,0:T(8,128)(2,1)} copy(bf16[1,2,1,512,512]{4,3,2,1,0:T(8,128)(2,1)} %bitcast.17) | data formatting | bytes 2097152
  120.2 0.0 copy-done
  120.2 0.0 copy-start.1
  120.2 0.7 copy.16
  120.9 0.2 copy-done.1
  121.1 0.6 copy.17
Async XLA Ops:
  117.9 2.3 %copy-start = (f32[3,16,1024]{2,1,0:T(8,128)S(1)}, f32[3,16,1024]{2,1,0:T(8,128)}, u32[]{:S(2)}) copy-start(f32[3,16,1024]{2,1,0:T(8,128)} %get-tuple-element.7) | copy-start | bytes 589828
  120.2 0.9 copy-start.1

commit v3 on v2

--- a/solution.py
+++ b/solution.py
@@ -126,6 +126,113 @@
     return tasks, order, clock
 
 
+def gather2(split, width, rows, rate, lag, ahead, wts):
+    sizes = {"z": NZ, "y": NY}
+    axes = (("z", "y"), ("y", "z"))
+    pieces = ((0, split), (split, width - split))
+    links = {(a, w): [] for a in "zy" for w in (1, -1)}
+    free = {k: 0.0 for k in links}
+    sends, order, events = [], [], []
+    tick = 0
+    def offer(now, group, axis, way, offset, piece):
+        nonlocal tick
+        if piece[1] == 0: return
+        reach = sizes[axis] // 2
+        gone = abs(offset[axis])
+        left = reach - gone
+        two = axes[group][1]
+        follow = sizes[two] // 2 if axis == axes[group][0] else 0
+        score = -(left * wts[0] + follow * wts[1])
+        tick += 1
+        heapq.heappush(links[(axis, way)], (score, tick, now, group, dict(offset), piece))
+    here = {"z": 0, "y": 0}
+    for group in (0, 1):
+        for axis in axes[group]:
+            for way in (1, -1):
+                offer(0.0, group, axis, way, here, pieces[group])
+    now = 0.0
+    last = 0.0
+    while True:
+        for key, queue in links.items():
+            while queue and free[key] <= now + ahead + 1e-6:
+                score, _, _, group, offset, piece = heapq.heappop(queue)
+                axis, way = key
+                begin = max(now, free[key])
+                free[key] = begin + rows * piece[1] * 2 / rate
+                ident = len(sends)
+                shift = dict(offset); shift[axis] = wrap(shift[axis] - way, sizes[axis])
+                sends.append((axis, way, dict(offset), shift, piece))
+                order.append(("send", ident))
+                heapq.heappush(events, (free[key] + lag, 0, ident, group))
+        nxt = [free[k] - ahead for k, q in links.items() if q]
+        t = min(nxt) if nxt else float("inf")
+        if events and events[0][0] <= t:
+            now, _, ident, group = heapq.heappop(events)
+            last = max(last, now)
+            axis, way, _, offset, piece = sends[ident]
+            order.append(("wait", ident))
+            reach = sizes[axis] // 2
+            done = abs(offset[axis])
+            if done < reach - 1: offer(now, group, axis, way, offset, piece)
+            elif done == reach - 1: offer(now, group, axis, way, offset, halves(piece)[0 if way > 0 else 1])
+            if axis == axes[group][0]:
+                for side in (1, -1): offer(now, group, axes[group][1], side, offset, piece)
+        elif nxt:
+            now = max(now, t)
+        else:
+            break
+    return sends, order, last
+
+
+def scatter2(split, width, rows, rate, lag, cost, ahead, wts):
+    tasks = scatter_plan(split, width, rows, rate, lag, cost)[0]
+    needs, users = {}, {}
+    for key, task in tasks.items():
+        deps = [("r", n) for n in task["recvs"]] + [("l", n) for n in task["locals"]]
+        needs[key] = len(deps)
+        for kind, n in deps:
+            users.setdefault((kind, n), []).append(key)
+    links = {(a, w): [] for a in "zy" for w in (1, -1)}
+    free = {k: 0.0 for k in links}
+    order, events = [], []
+    def remaining(key):
+        group, stage, way, j, o2 = key
+        return wts[0] * j + wts[1] * abs(o2) * (stage == 1)
+    def ready(key, now):
+        task = tasks[key]
+        if task["axis"] is None:
+            order.append(key)
+            heapq.heappush(events, (now + cost * rows * task["piece"][1], "l", key))
+        else:
+            heapq.heappush(links[(task["axis"], task["way"])], (-remaining(key), len(order), key))
+    now = 0.0
+    for key in tasks:
+        if needs[key] == 0: ready(key, 0.0)
+    last = 0.0
+    while True:
+        for link, queue in links.items():
+            while queue and free[link] <= now + ahead + 1e-6:
+                key = heapq.heappop(queue)[2]
+                begin = max(now, free[link])
+                free[link] = begin + rows * tasks[key]["piece"][1] * 2 / rate
+                order.append(key)
+                heapq.heappush(events, (free[link] + lag, "r", key))
+        nxt = [free[k] - ahead for k, q in links.items() if q]
+        t = min(nxt) if nxt else float("inf")
+        if events and events[0][0] <= t:
+            now, kind, key = heapq.heappop(events)
+            last = max(last, now)
+            for user in users.get((kind, key), []):
+                needs[user] -= 1
+                if needs[user] == 0: ready(user, now)
+        elif nxt:
+            now = max(now, t)
+        else:
+            break
+    assert len(order) == len(tasks)
+    return tasks, order, last
+
+
 F32, BF16 = jnp.float32, jnp.bfloat16
 MESH = pl.DeviceIdType.MESH
 SECTIONS = 8
@@ -156,7 +263,7 @@
 
 
 def kernel(gather, scatter, slots, x_hbm, top_hbm, skip_hbm, wc_hbm, wm_hbm, cot_hbm, conv_hbm, mix_hbm,
-           wc_v, w_v, x_v, xf_v, xt_v, ht_v, a1_v, a2_v, hs_v, pf_v, a_v, out_v, g_v,
+           w_v, x_v, xf_v, xt_v, ht_v, a1_v, a2_v, hs_v, pf_v, a_v, out_v, g_v,
            ra_v, rb_v, sa_v, sb_v,
            ag_send, ag_recv, rs_send, rs_recv, ch_send, ch_recv, ld_sem, st_sem):
     p = lax.axis_index("pipe")
@@ -178,10 +285,13 @@
     skip_load = pltpu.make_async_copy(skip_hbm, a_v.at[:, SKIP], ld_sem.at[1])
     top_load = pltpu.make_async_copy(top_hbm, a_v.at[:, RES], ld_sem.at[2])
     own = rows_at({"z": 0, "y": 0})
-    wc_load = pltpu.make_async_copy(wc_hbm, wc_v, ld_sem.at[3])
-    wm_load = pltpu.make_async_copy(wm_hbm, w_v.at[own, CONV:WIDTH], ld_sem.at[4])
-    wc_load.start()
-    wm_load.start()
+    own_loads = [
+        pltpu.make_async_copy(
+            wc_hbm.at[k] if k < 3 else wm_hbm, w_v.at[own, k * 1024:(k + 1) * 1024], ld_sem.at[3 + k])
+        for k in range(4)
+    ]
+    for load in own_loads:
+        load.start()
     x_load.start()
     skip_load.start()
 
@@ -197,11 +307,8 @@
     for way in (1, SECTIONS - 1):
         neighbour = {"pipe": lax.rem(p + way, SECTIONS)}
         pl.semaphore_signal(barrier, inc=1, device_id=neighbour, device_id_type=MESH)
-    wc_load.wait()
-    taps = wc_v[...].astype(F32)
-    for k in range(3):
-        w_v[own, k * 1024:(k + 1) * 1024] = taps[:, k, :].astype(BF16)
-    wm_load.wait()
+    for load in own_loads:
+        load.wait()
     pl.semaphore_wait(barrier, 6)
 
     ag_sends, ag_order, _ = gather
@@ -442,10 +549,10 @@
     x = x_ckpt.reshape(ROWS, C)
     top = top_cot.reshape(ROWS, C)
     skip = skip_cot.reshape(ROWS, C)
-    taps = w_conv.reshape(SHARD, 3, 2 * C)
+    taps = w_conv.reshape(SHARD, 3, 2 * C).transpose(1, 0, 2)
     mix = w_mix.reshape(SHARD, 2 * C)
-    gather = gather_plan(AG_SPLIT, WIDTH, SHARD, RATE, LAG)
-    scatter = scatter_plan(RS_SPLIT, WIDTH, SHARD, RATE, LAG, 2e-6)
+    gather = gather2(AG_SPLIT, WIDTH, SHARD, 53e3, 2.4, 0.0, (1, 1))
+    scatter = scatter2(RS_SPLIT, WIDTH, SHARD, 53e3, 2.4, 2e-6, 0.0, (1, 1))
     slots, counts, sems = {}, [0, 0], 0
     for key, task in scatter[0].items():
         if task["axis"] is not None:
@@ -465,7 +572,6 @@
         in_specs=[anywhere] * 5,
         out_specs=(anywhere,) * 3,
         scratch_shapes=[
-            pltpu.VMEM((SHARD, 3, 2 * C), BF16),
             pltpu.VMEM((C, WIDTH), BF16),
             pltpu.VMEM((ROWS, C), BF16),
             pltpu.VMEM((2 * STRIDE, C), F32),
@@ -483,7 +589,7 @@
             pltpu.VMEM((counts[0], SHARD, RS_SPLIT), BF16),
             pltpu.VMEM((counts[1], SHARD, WIDTH - RS_SPLIT), BF16),
             dma((sends,)), dma((sends,)), dma((sems,)), dma((sems,)),
-            dma((CHUNKS,)), dma((CHUNKS,)), dma((5,)), dma((CHUNKS,)),
+            dma((CHUNKS,)), dma((CHUNKS,)), dma((7,)), dma((CHUNKS,)),
         ],
         compiler_params=pltpu.CompilerParams(
             collective_id=0, has_side_effects=True, vmem_limit_bytes=67043328),

time: 122 us -> 115 us (0.943)
  Pallas kernels: 116 us -> 111 us
  local copies, waits for them, and re-layouts: 5.43 us -> 3.8 us
    pallas_call x1, Pallas kernels: 116 us -> 111 us  [local(): pl.pallas_call(functools.partial(kernel, gather, scatter, slots), out_sha...]
    unnamed x8 -> x7, local copies, waits for them, and re-layouts: 5.43 us -> 3.8 us
where the time goes in v3:
time: 115 us
  Pallas kernels  111 us (97%)
  local copies, waits for them, and re-layouts  3.8 us (3%)
    pallas_call x1, Pallas kernels, local(): pl.pallas_call(functools.partial(kernel, gather, scatter, slots), out_sha...  111 us
    unnamed x7, local copies, waits for them, and re-layouts  3.8 us

profile of v3, /device:TPU:8, one launch (start us, length us, event | category | flops | bytes accessed | tf_op | source)
XLA Modules:
  0.0 115.3 jit_solution(10293717548988757129)
XLA Ops:
  0.6 110.8 %shard_map.76 = (bf16[1024,512]{1,0:T(8,128)(2,1)}, f32[3,16,1024]{2,1,0:T(8,128)}, f32[16,1024]{1,0:T(8,128)}) custom-call(bf16[1024,512]{1,0:T(8,128)(2,1)} %bitcast.14, bf16[1024,512]{1,0:T(8,128)(2,1)} %bitcast.15, bf16[1024,512]{1,0:T(8,128)(2,1)} %bitcast.16, bf16[3,16,1024]{2,1,0:T(8,128)(2,1)} %bitcast.19, bf16[16,1024]{1,0:T(8,128)(2,1)} %bitcast.21), custom_call_target="tpu_custom_call" | custom-call | tf_op jit(solution)/shard_map/pallas_call | solution.py:565
  111.5 0.0 copy-start
  111.5 2.3 %copy.12 = bf16[1,2,1,512,512]{4,3,2,1,0:T(8,128)(2,1)} copy(bf16[1,2,1,512,512]{4,3,2,1,0:T(8,128)(2,1)} %bitcast.17) | data formatting | bytes 2097152
  113.8 0.0 copy-done
  113.8 0.0 copy-start.1
  113.8 0.7 copy.13
  114.5 0.2 copy-done.1
  114.7 0.6 copy.14
Async XLA Ops:
  111.5 2.3 %copy-start = (f32[3,16,1024]{2,1,0:T(8,128)S(1)}, f32[3,16,1024]{2,1,0:T(8,128)}, u32[]{:S(2)}) copy-start(f32[3,16,1024]{2,1,0:T(8,128)} %get-tuple-element.7) | copy-start | bytes 589828
  113.8 0.9 copy-start.1

commit v4 on v3

--- a/solution.py
+++ b/solution.py
@@ -244,8 +244,11 @@
 CONV = 3072
 RES = slice(3072, 3584)
 SKIP = slice(3584, 4096)
-CHUNK = 256
+CHUNK = 128
+AHEAD = 256
 CHUNKS = ROWS // CHUNK
+AHEADS = ROWS // AHEAD
+RATIO = AHEAD // CHUNK
 PER_SEQ = LEN // CHUNK
 PAD = 264
 STRIDE = LEN + PAD
@@ -263,7 +266,7 @@
 
 
 def kernel(gather, scatter, slots, x_hbm, top_hbm, skip_hbm, wc_hbm, wm_hbm, cot_hbm, conv_hbm, mix_hbm,
-           w_v, x_v, xf_v, xt_v, ht_v, a1_v, a2_v, hs_v, pf_v, a_v, out_v, g_v,
+           w_v, wt_v, x_v, xf_v, xt_v, ht_v, a1_v, a2_v, hs_v, pf_v, a_v, out_v, g_v,
            ra_v, rb_v, sa_v, sb_v,
            ag_send, ag_recv, rs_send, rs_recv, ch_send, ch_recv, ld_sem, st_sem):
     p = lax.axis_index("pipe")
@@ -346,29 +349,30 @@
 
     d = (1 + lax.rem(p, 2)) * (1 + 3 * lax.rem(p // 2, 2)) * (1 + 15 * (p // 4))
 
-    def shifted(ref, base, down):
-        window = ref[pl.ds(pl.multiple_of(base, 8), CHUNK + 8), :]
+    def shifted(ref, base, down, size):
+        window = ref[pl.ds(pl.multiple_of(base, 8), size + 8), :]
         width = window.shape[1]
-        turned = pltpu.roll(window.reshape(CHUNK // 8 + 1, 8, width), down, 1)
-        inner = lax.broadcasted_iota(jnp.int32, (CHUNK // 8, 8, width), 1) >= down
-        return jnp.where(inner, turned[1:], turned[:-1]).reshape(CHUNK, width).astype(BF16)
+        turned = pltpu.roll(window.reshape(size // 8 + 1, 8, width), down, 1)
+        inner = lax.broadcasted_iota(jnp.int32, (size // 8, 8, width), 1) >= down
+        return jnp.where(inner, turned[1:], turned[:-1]).reshape(size, width).astype(BF16)
 
     def delayed(s, t, shift):
         down = lax.rem(shift, 8)
-        return shifted(xf_v, s * STRIDE + PAD + t - (shift - down) - 8, down)
+        return shifted(xf_v, s * STRIDE + PAD + t - (shift - down) - 8, down, AHEAD)
 
     def advanced(s, t, shift):
         down = lax.rem(8 - lax.rem(shift, 8), 8)
-        return shifted(pf_v, s * STRIDE + t + (shift + down) - 8, down)
-
-    def place(q):
-        s = q // PER_SEQ
-        t = (PER_SEQ - 1 - lax.rem(q, PER_SEQ)) * CHUNK
-        row = pl.multiple_of(s * LEN + t, CHUNK)
-        return s, t, pl.ds(row, CHUNK)
+        return shifted(pf_v, s * STRIDE + t + (shift + down) - 8, down, CHUNK)
+
+    def place(q, size):
+        per = LEN // size
+        s = q // per
+        t = (per - 1 - lax.rem(q, per)) * size
+        row = pl.multiple_of(s * LEN + t, size)
+        return s, t, pl.ds(row, size)
 
     def forward(q):
-        s, t, rows = place(q)
+        s, t, rows = place(q, AHEAD)
         x0 = x_v[rows, :]
         pre = dot(x0, w_v[:, 0:1024])
         pre = pre + dot(delayed(s, t, d), w_v[:, 1024:2048])
@@ -386,37 +390,44 @@
         forward(q)
         return carry
 
-    lax.fori_loop(0, jnp.where(is_last, 1, CHUNKS), forward_step, 0)
+    lax.fori_loop(0, jnp.where(is_last, 1, AHEADS), forward_step, 0)
+
+    def turn_step(n, carry):
+        lanes = pl.ds(pl.multiple_of(n * C, C), C)
+        wt_v[lanes, :] = w_v[:, lanes].T
+        return carry
+
+    lax.fori_loop(0, (CONV + C) // C, turn_step, 0)
 
     @pl.when(is_last)
     def _():
         top_load.wait()
 
     def chain_send(q):
-        _, _, rows = place(q)
+        _, _, rows = place(q, CHUNK)
         return pltpu.make_async_remote_copy(
             out_v.at[rows, :], a_v.at[rows, RES], ch_send.at[q], ch_recv.at[q],
             device_id={"pipe": p - 1}, device_id_type=MESH)
 
     def chain_recv(q):
-        _, _, rows = place(q)
+        _, _, rows = place(q, CHUNK)
         return pltpu.make_async_remote_copy(
             a_v.at[rows, RES], a_v.at[rows, RES], ch_send.at[q], ch_recv.at[q],
             device_id={"pipe": p + 1}, device_id_type=MESH)
 
     def chain_store(q):
-        _, _, rows = place(q)
+        _, _, rows = place(q, CHUNK)
         return pltpu.make_async_copy(out_v.at[rows, :], cot_hbm.at[rows, :], st_sem.at[q])
 
     def chain_step(q, carry):
-        s, t, rows = place(q)
+        s, t, rows = place(q, CHUNK)
 
         @pl.when(jnp.logical_not(is_last))
         def _():
             chain_recv(q).wait_recv()
 
         g = a_v[rows, RES]
-        hg = hs_v[rows, :] + dot_nt(g, w_v[:, RES])
+        hg = hs_v[rows, :] + dot(g, wt_v[CONV:, :])
         pg1 = (hg * a1_v[rows, :]).astype(BF16)
         pg2 = (hg * a2_v[rows, :]).astype(BF16)
         a_v[rows, 0:C] = pg1
@@ -426,7 +437,7 @@
         pf_v[prow, C:2 * C] = pg2.astype(F32)
         a_v[rows, 1024:2048] = advanced(s, t, d)
         a_v[rows, 2048:3072] = advanced(s, t, 2 * d)
-        out = g.astype(F32) + dot_nt(a_v[rows, 0:CONV], w_v[:, 0:CONV])
+        out = g.astype(F32) + dot(a_v[rows, 0:CONV], wt_v[0:CONV, :])
         out_v[rows, :] = out.astype(BF16)
 
         @pl.when(jnp.logical_not(is_first))
@@ -435,9 +446,11 @@
 
         chain_store(q).start()
 
-        @pl.when(jnp.logical_and(is_last, q < CHUNKS - 1))
+        more = jnp.logical_and(lax.rem(q, RATIO) == RATIO - 1, q < CHUNKS - 1)
+
+        @pl.when(jnp.logical_and(is_last, more))
         def _():
-            forward(jnp.minimum(q + 1, CHUNKS - 1))
+            forward(jnp.minimum((q + 1) // RATIO, AHEADS - 1))
 
         return carry
 
@@ -573,6 +586,7 @@
         out_specs=(anywhere,) * 3,
         scratch_shapes=[
             pltpu.VMEM((C, WIDTH), BF16),
+            pltpu.VMEM((CONV + C, C), BF16),
             pltpu.VMEM((ROWS, C), BF16),
             pltpu.VMEM((2 * STRIDE, C), F32),
             pltpu.VMEM((C, ROWS), BF16),

time: 115 us -> 110 us (0.957)
  Pallas kernels: 111 us -> 106 us
    pallas_call x1, Pallas kernels: 111 us -> 106 us  [local(): pl.pallas_call(functools.partial(kernel, gather, scatter, slots), out_sha...]
where the time goes in v4:
time: 110 us
  Pallas kernels  106 us (96%)
  local copies, waits for them, and re-layouts  3.8 us (3%)
    pallas_call x1, Pallas kernels, local(): pl.pallas_call(functools.partial(kernel, gather, scatter, slots), out_sha...  106 us
    unnamed x7, local copies, waits for them, and re-layouts  3.8 us

profile of v4, /device:TPU:8, one launch (start us, length us, event | category | flops | bytes accessed | tf_op | source)
XLA Modules:
  0.0 110.3 jit_solution(13512271340272477292)
XLA Ops:
  0.6 105.9 %shard_map.76 = (bf16[1024,512]{1,0:T(8,128)(2,1)}, f32[3,16,1024]{2,1,0:T(8,128)}, f32[16,1024]{1,0:T(8,128)}) custom-call(bf16[1024,512]{1,0:T(8,128)(2,1)} %bitcast.14, bf16[1024,512]{1,0:T(8,128)(2,1)} %bitcast.15, bf16[1024,512]{1,0:T(8,128)(2,1)} %bitcast.16, bf16[3,16,1024]{2,1,0:T(8,128)(2,1)} %bitcast.19, bf16[16,1024]{1,0:T(8,128)(2,1)} %bitcast.21), custom_call_target="tpu_custom_call" | custom-call | tf_op jit(solution)/shard_map/pallas_call | solution.py:578
  106.5 0.0 copy-start
  106.5 2.3 %copy.12 = bf16[1,2,1,512,512]{4,3,2,1,0:T(8,128)(2,1)} copy(bf16[1,2,1,512,512]{4,3,2,1,0:T(8,128)(2,1)} %bitcast.17) | data formatting | bytes 2097152
  108.8 0.0 copy-done
  108.8 0.0 copy-start.1
  108.8 0.7 copy.13
  109.5 0.2 copy-done.1
  109.7 0.6 copy.14
Async XLA Ops:
  106.5 2.3 %copy-start = (f32[3,16,1024]{2,1,0:T(8,128)S(1)}, f32[3,16,1024]{2,1,0:T(8,128)}, u32[]{:S(2)}) copy-start(f32[3,16,1024]{2,1,0:T(8,128)} %get-tuple-element.7) | copy-start | bytes 589828
  108.8 0.9 copy-start.1

commit v5 on v4

--- a/solution.py
+++ b/solution.py
@@ -558,6 +558,24 @@
         store.wait()
 
 
+def hand_out(cot_in, conv_in, mix_in, cot_out, conv_out, mix_out, cot_v, conv_v, mix_v, load_sem, store_sem):
+    quarter = ROWS // 4
+    parts = [
+        tuple(ref.at[pl.ds(k * quarter, quarter)] for ref in (cot_in, cot_v, cot_out)) for k in range(4)
+    ] + [(conv_in, conv_v, conv_out), (mix_in, mix_v, mix_out)]
+    moves = []
+    for k, part in enumerate(parts):
+        source, middle, target = part
+        load = pltpu.make_async_copy(source, middle, load_sem.at[k])
+        load.start()
+        moves.append((load, pltpu.make_async_copy(middle, target, store_sem.at[k])))
+    for load, store in moves:
+        load.wait()
+        store.start()
+    for _, store in moves:
+        store.wait()
+
+
 def local(x_ckpt, top_cot, skip_cot, w_conv, w_mix):
     x = x_ckpt.reshape(ROWS, C)
     top = top_cot.reshape(ROWS, C)
@@ -608,6 +626,15 @@
         compiler_params=pltpu.CompilerParams(
             collective_id=0, has_side_effects=True, vmem_limit_bytes=67043328),
     )(x, top, skip, taps, mix)
+    results = (cot, conv_grad, mix_grad)
+    cot, conv_grad, mix_grad = pl.pallas_call(
+        hand_out,
+        out_shape=tuple(jax.ShapeDtypeStruct(r.shape, r.dtype) for r in results),
+        in_specs=[anywhere] * 3,
+        out_specs=(anywhere,) * 3,
+        scratch_shapes=[pltpu.VMEM(r.shape, r.dtype) for r in results] + [dma((6,)), dma((6,))],
+        compiler_params=pltpu.CompilerParams(vmem_limit_bytes=67043328),
+    )(*results)
     return (
         cot.reshape(x_ckpt.shape),
         conv_grad.transpose(1, 0, 2).reshape(w_conv.shape),

time: 110 us -> 109 us (level)
  local copies, waits for them, and re-layouts: 3.8 us -> 0 us
  Pallas kernels: 106 us -> 108 us
    unnamed x7 -> x0, local copies, waits for them, and re-layouts: 3.8 us -> none
    pallas_call x0 -> x1, Pallas kernels: none -> 2.09 us  [local(): pl.pallas_call(hand_out, out_shape=tuple((jax.ShapeDtypeStruct(r.shape, r...]
where the time goes in v5:
time: 109 us
  Pallas kernels  108 us (99%)
    pallas_call x1, Pallas kernels, local(): pl.pallas_call(functools.partial(kernel, gather, scatter, slots), out_sha...  106 us

profile of v5, /device:TPU:8, one launch (start us, length us, event | category | flops | bytes accessed | tf_op | source)
XLA Modules:
  0.0 108.6 jit_solution(5641289053084259986)
XLA Ops:
  0.6 105.9 %shard_map.76 = (bf16[1024,512]{1,0:T(8,128)(2,1)}, f32[3,16,1024]{2,1,0:T(8,128)}, f32[16,1024]{1,0:T(8,128)}) custom-call(bf16[1024,512]{1,0:T(8,128)(2,1)} %bitcast.14, bf16[1024,512]{1,0:T(8,128)(2,1)} %bitcast.15, bf16[1024,512]{1,0:T(8,128)(2,1)} %bitcast.16, bf16[3,16,1024]{2,1,0:T(8,128)(2,1)} %bitcast.17, bf16[16,1024]{1,0:T(8,128)(2,1)} %bitcast.18), custom_call_target="tpu_custom_call" | custom-call | tf_op jit(solution)/shard_map/pallas_call | solution.py:596
  106.5 2.1 %shard_map.77 = (bf16[1024,512]{1,0:T(8,128)(2,1)}, f32[3,16,1024]{2,1,0:T(8,128)}, f32[16,1024]{1,0:T(8,128)}) custom-call(bf16[1024,512]{1,0:T(8,128)(2,1)} %get-tuple-element.9.cot_in, f32[3,16,1024]{2,1,0:T(8,128)} %get-tuple-element.10.conv_in, f32[16,1024]{1,0:T(8,128)} %get-tuple-element.11.mix_in), custom_call_target="tpu_custom_call" | custom-call | tf_op jit(solution)/shard_map/pallas_call | solution.py:630
